TPU v7x, 128 devices: a whole 4x4x4 slice. The times are simulated.
128 devices in a mesh: grp: 8 (over y, core), dom: 16 (over z, x).
Axes of the slice: x: 4, y: 4, z: 4, core: 2. Of those that a mesh axis runs over, the one named last changes fastest.
Arguments:
- diag_blocks: bfloat16 [2048, 384, 384], P(('grp', 'dom')), may hold values from -0.3125 to 0.3125
- face_in: bfloat16 [4096, 384, 384], P(('grp', 'dom')), may hold values from -0.3125 to 0.3125
- face_cross: bfloat16 [2048, 384, 384], P(('grp', 'dom')), may hold values from -0.3125 to 0.3125
- metric: float32 [2048, 384], P(('grp', 'dom')), may hold values from 0.5 to 2
- source_in: int32 [4096], P(('grp', 'dom')), may hold values from 0 to 15
- source_cross: int32 [2048], P(('grp', 'dom')), may hold values from 0 to 15
- orient_in: int32 [4096], P(('grp', 'dom')), may hold values from 0 to 7
- orient_cross: int32 [2048], P(('grp', 'dom')), may hold values from 0 to 7
- peer_in: int32 [4096, 1], P(('grp', 'dom')), may hold values from 0 to 15; in each aligned block of 32 rows (0 to 31, 32 to 63, ...) at most 3 rows name the same one
- peer_cross: int32 [2048, 1], P(('grp', 'dom')), may hold values from 0 to 7; in each aligned block of 16 rows (0 to 15, 16 to 31, ...) at most 3 rows name the same one
- target_in: int32 [4096], P(('grp', 'dom')), may hold values from 0 to 47
- target_cross: int32 [2048], P(('grp', 'dom')), may hold values from 0 to 47
Outputs:
- coarse_diag: float32 [2048, 2304], P('grp')
- coarse_face: float32 [2048, 6912], P('grp')
Inputs may be any that keep to these rules, and one draw needn't show every extreme that they name: `peer_in`: at most 3 records of one device name the same partition; on some device exactly 3 do. `peer_cross`: at most 3 records of one device name the same group; on some device exactly 3 do.
All inputs are finite; a program needn't handle non-finite values.
Results may differ from a plain program's by a relative error of at most 0.0052.
Values may be sent and summed in bfloat16 or wider, within the bound.
A program may use at most 128 MiB of HBM per device.

v0:
```python
import jax
import jax.numpy as jnp
from jax import lax
from jax.sharding import PartitionSpec as P

CROSS_CAP = 3


def corner_table(var_count):
    nodes = -1.0 + 2.0 * jnp.arange(4, dtype=jnp.float32) / 3.0
    basis = jnp.stack(((1.0 - nodes) / 2.0, (1.0 + nodes) / 2.0), axis=1)
    cube = jnp.einsum("ia,jb,kc->abcijk", basis, basis, basis).reshape(8, 64)
    return jnp.kron(jnp.eye(var_count, dtype=jnp.float32), cube)


def restrictor(weights, orient):
    var_count = weights.shape[1] // 64
    table = corner_table(var_count)
    full = weights[:, None, :] * table[None]
    shaped = full.reshape(weights.shape[0], var_count * 8, var_count, 4, 4, 4)
    bits = orient.reshape(-1, 1, 1, 1, 1, 1)
    shaped = jnp.where(bits % 2 == 1, jnp.flip(shaped, 3), shaped)
    shaped = jnp.where(bits // 2 % 2 == 1, jnp.flip(shaped, 4), shaped)
    shaped = jnp.where(bits // 4 % 2 == 1, jnp.flip(shaped, 5), shaped)
    return shaped.reshape(weights.shape[0], var_count * 8, var_count * 64).astype(jnp.bfloat16)


def plain_restrictor(weights):
    table = corner_table(weights.shape[1] // 64)
    return (weights[:, None, :] * table[None]).astype(jnp.bfloat16)


def pick_rows(index, table):
    picks = (index[:, None] == jnp.arange(table.shape[0], dtype=jnp.int32)[None, :]).astype(
        jnp.float32
    )
    return jnp.dot(picks, table, precision=lax.Precision.HIGHEST)


def one_sided(blocks, column_side):
    return jnp.einsum(
        "rcj,rij->rci", column_side, blocks, preferred_element_type=jnp.float32
    ).astype(jnp.bfloat16)


def coarse_terms(row_side, products):
    return jnp.einsum("rci,rdi->rcd", row_side, products, preferred_element_type=jnp.float32)


def id_row(values, width):
    flat = values.reshape(-1).astype(jnp.bfloat16)
    return jnp.pad(flat, (0, width - flat.shape[0]))[None, :]


def per_device(
    diag_blocks,
    face_in,
    face_cross,
    metric,
    source_in,
    source_cross,
    orient_in,
    orient_cross,
    peer_in,
    peer_cross,
    target_in,
    target_cross,
):
    elem_count = metric.shape[0]
    coarse_width = metric.shape[1] // 8
    square = coarse_width * coarse_width
    slots_dev = 3 * elem_count
    group_width = lax.axis_size("dom")
    group_count = lax.axis_size("grp")
    my_dom = lax.axis_index("dom")
    my_grp = lax.axis_index("grp")
    inner_count = face_in.shape[0]
    cross_count = face_cross.shape[0]
    metric_dom = lax.all_gather(metric, "dom", axis=0, tiled=True)
    metric_grp = lax.all_gather(metric, "grp", axis=0, tiled=True)
    diag_side = plain_restrictor(metric)
    diag_c = coarse_terms(diag_side, one_sided(diag_blocks, diag_side))
    diag_rows = diag_c.reshape(elem_count, square).astype(jnp.bfloat16)
    diag_all = lax.all_gather(diag_rows, "dom", axis=0, tiled=True)
    cross_y = one_sided(face_cross, restrictor(pick_rows(source_cross, metric), orient_cross))
    peer_x = peer_cross[:, 0]
    cross_row_side = plain_restrictor(
        pick_rows(peer_x * elem_count + target_cross // 3, metric_grp)
    )
    cross_c = coarse_terms(cross_row_side, cross_y).reshape(cross_count, square)
    cross_ids = jnp.stack((peer_x, target_cross), axis=1)
    cross_packet = jnp.concatenate(
        (cross_c.astype(jnp.bfloat16), id_row(cross_ids, square)), axis=0
    )
    cross_got = lax.all_gather(cross_packet, "grp", axis=0)
    got_rows = cross_got[:, :cross_count, :]
    got_ids = cross_got[:, cross_count, : 2 * cross_count].astype(jnp.int32)
    got_peer = got_ids[:, 0::2]
    got_target = got_ids[:, 1::2]
    match = got_peer == my_grp
    rank = jnp.cumsum(match.astype(jnp.int32), axis=1) - 1
    picks = match[:, None, :] & (
        rank[:, None, :] == jnp.arange(CROSS_CAP, dtype=jnp.int32)[None, :, None]
    )
    mine_rows = (
        jnp.einsum(
            "skr,srq->skq", picks.astype(jnp.bfloat16), got_rows, preferred_element_type=jnp.float32
        )
        .astype(jnp.bfloat16)
        .reshape(group_count * CROSS_CAP, square)
    )
    mine_target = jnp.sum(jnp.where(picks, got_target[:, None, :], 0), axis=2)
    mine_slot = jnp.where(jnp.any(picks, axis=2), my_dom * slots_dev + mine_target, -1).reshape(-1)
    inner_y = one_sided(face_in, restrictor(pick_rows(source_in, metric), orient_in))
    peer_i = peer_in[:, 0]
    inner_row_side = plain_restrictor(pick_rows(peer_i * elem_count + target_in // 3, metric_dom))
    inner_c = coarse_terms(inner_row_side, inner_y).reshape(inner_count, square)
    inner_slot = peer_i * slots_dev + target_in
    slots = jnp.concatenate((inner_slot, mine_slot), axis=0)
    valid = slots >= 0
    slot_code = jnp.stack(
        (jnp.where(valid, slots // 32, -1), jnp.where(valid, slots % 32, 0)), axis=1
    )
    face_packet = jnp.concatenate(
        (inner_c.astype(jnp.bfloat16), mine_rows, id_row(slot_code, square)), axis=0
    )
    face_all = lax.all_gather(face_packet, "dom", axis=0)
    contrib_count = slots.shape[0]
    contrib = face_all[:, :contrib_count, :].reshape(group_width * contrib_count, square)
    codes = face_all[:, contrib_count, : 2 * contrib_count].astype(jnp.int32)
    hi = codes[:, 0::2].reshape(-1)
    lo = codes[:, 1::2].reshape(-1)
    got_slot = jnp.where(hi >= 0, hi * 32 + lo, -1)
    group_slots = group_width * slots_dev
    onehot = (jnp.arange(group_slots, dtype=jnp.int32)[:, None] == got_slot[None, :]).astype(
        jnp.bfloat16
    )
    face = jnp.dot(onehot, contrib, preferred_element_type=jnp.float32)
    coarse_diag = diag_all.astype(jnp.float32)
    coarse_face = face.reshape(group_width * elem_count, 3 * square)
    return (coarse_diag, coarse_face)


def solution(mesh):
    placed = (
        P(("grp", "dom"), None, None),
        P(("grp", "dom"), None, None),
        P(("grp", "dom"), None, None),
        P(("grp", "dom"), None),
        P(("grp", "dom")),
        P(("grp", "dom")),
        P(("grp", "dom")),
        P(("grp", "dom")),
        P(("grp", "dom"), None),
        P(("grp", "dom"), None),
        P(("grp", "dom")),
        P(("grp", "dom")),
    )
    return jax.shard_map(
        per_device,
        mesh=mesh,
        in_specs=placed,
        out_specs=(P("grp", None), P("grp", None)),
        check_vma=False,
    )
```

profile of v0, /device:TPU:1, one launch (start us, length us, event | category | flops | bytes accessed | tf_op | source)
XLA Modules:
  0.0 171.8 jit_solution(11630039760645675383)
XLA Ops:
  7.4 0.1 mul.188
  7.5 0.1 broadcast_multiply_fusion.3
  7.6 0.1 mul.191
  7.8 4.3 %fusion.26 = bf16[16,48,48]{2,1,0:T(8,128)(2,1)S(1)} fusion(bf16[16,384,384]{2,1,0:T(8,128)(2,1)} %param.12, f32[48,384]{1,0:T(8,128)S(1)} %mul.191, f32[16,384]{1,0:T(8,128)} %param.15), kind=kOutput, calls=%fused_computation.30 | convolution fusion | flops 256315392 | bytes 4890624 | tf_op jit(solution)/shard_map/rci,rdi->rcd/dot_general | solution.py:47
  12.0 0.9 convert_element_type.104
  13.1 0.1 copy.31
  13.2 14.6 %all_gather.23 = f32[128,384]{1,0:T(8,128)S(1)} all-gather(f32[16,384]{1,0:T(8,128)S(1)} %copy-done), channel_id=1, replica_groups=mesh['grp'=8,'dom'=16] {'grp'}, dimensions={0}, use_global_device_ids=true | all-gather | bytes 221184 | tf_op jit(solution)/shard_map/all_gather | solution.py:80
  27.8 0.1 mul.206
  28.1 0.4 fusion.43
  28.6 1.0 broadcast_multiply_fusion.1
  29.6 0.6 reverse_select_fusion.5
  30.2 0.7 reverse_select_fusion.4
  30.9 0.7 fusion.1
  31.6 0.2 fusion.42
  31.8 4.3 %fusion.27 = bf16[16,48,48]{2,1,0:T(8,128)(2,1)S(1)} fusion(bf16[16,384,384]{2,1,0:T(8,128)(2,1)} %param.14, bf16[16,48,384]{1,0,2:T(8,128)(2,1)S(1)} %bitcast.38, f32[16,384]{1,0:T(8,128)S(1)} %fusion.42, f32[48,384]{1,0:T(8,128)S(1)} %mul.191), kind=kOutput, calls=%fused_computation.31 | convolution fusion | flops 255725568 | bytes 5480448 | tf_op jit(solution)/shard_map/rci,rdi->rcd/dot_general | solution.py:47
  36.1 0.2 convert_element_type.117
  36.3 0.1 copy.36
  36.4 0.1 convert_element_type.118
  36.6 13.5 %all-gather.2 = bf16[8,17,2304]{2,1,0:T(8,128)(2,1)S(1)} all-gather(bf16[1,17,2304]{2,1,0:T(8,128)(2,1)S(1)} %maximum_bitcast_fusion.1), channel_id=2, replica_groups=mesh['grp'=8,'dom'=16] {'grp'}, dimensions={0}, use_global_device_ids=true | all-gather | bytes 705024 | tf_op jit(solution)/shard_map/all_gather | solution.py:95
  50.1 0.1 slice.25
  50.2 0.1 slice.27
  50.3 0.2 reduce_window_sum.11
  50.5 0.2 fusion.60
  50.7 0.2 convolution_convert_fusion
  50.9 20.3 %all_gather.22 = f32[256,384]{1,0:T(8,128)S(1)} all-gather(f32[16,384]{1,0:T(8,128)S(1)} %copy-done), channel_id=1, replica_groups=mesh['grp'=8,'dom'=16] {'dom'}, dimensions={0}, use_global_device_ids=true | all-gather | bytes 417792 | tf_op jit(solution)/shard_map/all_gather | solution.py:79
  71.2 0.2 select_reduce_fusion
  71.5 0.1 fusion.47
  71.6 0.1 copy.37
  71.7 0.1 convert_element_type.123
  71.9 0.1 reshape.525
  72.0 0.4 fusion.39
  72.4 1.9 %broadcast_multiply_fusion = bf16[32,48,6,4,4,4]{1,0,5,4,3,2:T(8,128)(2,1)S(1)} fusion(f32[48,6,4,4,4]{0,4,3,2,1:T(4,128)S(1)} %broadcast_multiply_fusion.2, f32[32,6,4,4,4]{0,4,3,2,1:T(4,128)S(1)} %bitcast.40), kind=kLoop, calls=%fused_computation.11 | loop fusion | flops 1179648 | bytes 1302528 | tf_op jit(solution)/shard_map/mul | solution.py:19
  74.4 0.3 fusion.37
  74.7 1.3 reverse_select_fusion.2
  76.0 1.5 reverse_select_fusion.1
  77.5 1.1 fusion
  78.6 8.9 %fusion.17 = bf16[32,48,48]{2,1,0:T(8,128)(2,1)} fusion(bf16[32,384,384]{2,1,0:T(8,128)(2,1)} %param.13, bf16[32,48,384]{1,0,2:T(8,128)(2,1)S(1)} %bitcast.37, f32[48,384]{1,0:T(8,128)S(1)} %mul.191, f32[32,384]{1,0:T(8,128)S(1)} %fusion.37), kind=kOutput, calls=%fused_computation.23 | convolution fusion | flops 511451136 | bytes 10887168 | tf_op jit(solution)/shard_map/rci,rdi->rcd/dot_general | solution.py:47
  87.5 1.4 convert_element_type.111
  88.9 0.7 maximum_bitcast_fusion
  89.7 2.8 %convert_element_type.105 = f32[256,2304]{1,0:T(8,128)} convert(bf16[256,2304]{1,0:T(8,128)(2,1)} %all-gather.7.cloned.1.call-done) | non-fusion elementwise | flops 589824 | bytes 3538944 | tf_op jit(solution)/shard_map/convert_element_type | solution.py:139
  92.5 54.4 %all-gather.9.cloned.1.call-done = bf16[16,57,2304]{2,1,0:T(8,128)(2,1)} async-done(((bf16[1,57,2304]{2,1,0:T(8,128)(2,1)}), bf16[16,57,2304]{2,1,0:T(8,128)(2,1)}) %all-gather.9.cloned.1.call-update) | async-done | bytes 4202512 | tf_op jit(solution)/shard_map/all_gather | solution.py:127
  146.9 0.8 slice_convert_fusion
  147.7 0.2 slice.29
  147.9 0.2 slice.30
  148.1 0.1 select_n.198
  148.2 2.2 %slice-done = bf16[16,56,2304]{2,1,0:T(8,128)(2,1)S(1)} async-done(((bf16[16,57,2304]{2,1,0:T(8,128)(2,1)}), bf16[16,56,2304]{2,1,0:T(8,128)(2,1)S(1)}, s32[]{:S(2)}) %slice-start) | async-done | bytes 4128792 | tf_op jit(solution)/shard_map/slice | solution.py:129
  150.4 6.0 %fusion.4 = f32[768,2304]{1,0:T(8,128)} fusion(bf16[896,2304]{1,0:T(8,128)(2,1)S(1)} %bitcast.39, s32[896]{0:T(1024)S(1)} %select_n.198), kind=kOutput, calls=%fused_computation.13 | convolution fusion | flops 3171581952 | bytes 11210240 | tf_op jit(solution)/shard_map/dot_general | solution.py:138
  156.3 8.6 %reshape.527 = f32[256,6912]{1,0:T(8,128)} reshape(f32[768,2304]{1,0:T(8,128)} %fusion.4) | data formatting | bytes 14155776 | tf_op jit(solution)/shard_map/reshape | solution.py:140
  (52 shorter events, 0.9 us)
Async XLA Ops:
  7.2 6.0 %copy-start = (f32[16,384]{1,0:T(8,128)S(1)}, f32[16,384]{1,0:T(8,128)}, u32[]{:S(2)}) copy-start(f32[16,384]{1,0:T(8,128)} %param.15) | copy-start | bytes 73732
  7.2 82.5 %all-gather.7.cloned.1.call-start = ((), (), s32[]{:S(2)}) async-start(), calls=%async_computation | async-start | bytes 1253376 | tf_op jit(solution)/shard_map/all_gather | solution.py:84
  7.7 20.4 %copy-start.1 = (s32[16]{0:T(128)S(1)}, s32[16]{0:T(128)}, u32[]{:S(2)}) copy-start(s32[16]{0:T(128)} %param.17) | copy-start | bytes 196
  7.7 20.7 %copy-start.3 = (s32[16]{0:T(128)S(1)}, s32[16]{0:T(128)}, u32[]{:S(2)}) copy-start(s32[16]{0:T(128)} %param.19) | copy-start | bytes 196
  7.7 20.7 %copy-start.5 = (s32[16,1]{0,1:T(1,128)S(1)}, s32[16,1]{0,1:T(1,128)}, u32[]{:S(2)}) copy-start(s32[16,1]{0,1:T(1,128)} %param.21) | copy-start | bytes 196
  7.8 20.8 %copy-start.4 = (s32[16]{0:T(128)S(1)}, s32[16]{0:T(128)}, u32[]{:S(2)}) copy-start(s32[16]{0:T(128)} %param.23) | copy-start | bytes 196
  12.9 134.0 %all-gather.9.cloned.1.call-start = ((), (), s32[]{:S(2)}) async-start(), calls=%async_computation.1 | async-start | bytes 5013504 | tf_op jit(solution)/shard_map/all_gather | solution.py:127
  31.8 39.7 %copy-start.6 = (s32[32]{0:T(128)S(1)}, s32[32]{0:T(128)}, u32[]{:S(2)}) copy-start(s32[32]{0:T(128)} %param.22) | copy-start | bytes 388
  31.8 39.7 %copy-start.7 = (s32[32,1]{0,1:T(1,128)S(1)}, s32[32,1]{0,1:T(1,128)}, u32[]{:S(2)}) copy-start(s32[32,1]{0,1:T(1,128)} %param.20) | copy-start | bytes 388
  31.8 40.2 %copy-start.2 = (s32[32]{0:T(128)S(1)}, s32[32]{0:T(128)}, u32[]{:S(2)}) copy-start(s32[32]{0:T(128)} %param.16) | copy-start | bytes 388
  36.6 37.8 %copy-start.8 = (s32[32]{0:T(128)S(1)}, s32[32]{0:T(128)}, u32[]{:S(2)}) copy-start(s32[32]{0:T(128)} %param.18) | copy-start | bytes 388
  148.2 2.2 %slice-start = ((bf16[16,57,2304]{2,1,0:T(8,128)(2,1)}), bf16[16,56,2304]{2,1,0:T(8,128)(2,1)S(1)}, s32[]{:S(2)}) async-start(bf16[16,57,2304]{2,1,0:T(8,128)(2,1)} %all-gather.9.cloned.1.call-done), calls=%async_computation.2 | async-start | bytes 8257536 | tf_op jit(solution)/shard_map/slice | solution.py:129
Sparse Core Ops, SparseCore 0:
  13.0 44.4 all-gather.6
  89.8 57.1 all-gather.8
where the time goes:
time: 172 us
  waiting for transfers between devices  54.5 us (32%)
  blocking collectives  48.4 us (28%)
  matrix products  24.8 us (14%)
  local copies, waits for them, and re-layouts  15.2 us (9%)
  between operations  14.4 us (8%)
  other arithmetic  14.3 us (8%)
    all_gather x1, waiting for transfers between devices, per_device(): face_all = lax.all_gather(face_packet, 'dom', axis=0)  54.4 us
    all_gather x1, blocking collectives, per_device(): metric_dom = lax.all_gather(metric, 'dom', axis=0, tiled=True)  20.3 us
    dot_general x3, matrix products, coarse_terms(): jnp.einsum('rci,rdi->rcd', row_side, products, preferred_element_type=jnp...  17.4 us
    all_gather x1, blocking collectives, per_device(): metric_grp = lax.all_gather(metric, 'grp', axis=0, tiled=True)  14.6 us
    all_gather x1, blocking collectives, per_device(): cross_got = lax.all_gather(cross_packet, 'grp', axis=0)  13.5 us
    reshape x1, local copies, waits for them, and re-layouts, per_device(): coarse_face = face.reshape(group_width * elem_count, 3 * square)  8.64 us
    dot_general x1, matrix products, per_device(): face = jnp.dot(onehot, contrib, preferred_element_type=jnp.float32)  5.97 us
  transfers between devices with their start and end apart: 2, of which 1 were waited for; matrix products, arithmetic and copies ran while one was open for 18% of the time, Pallas kernels for 0%

commit v1 on v0

--- a/solution.py
+++ b/solution.py
@@ -77,7 +77,8 @@
     inner_count = face_in.shape[0]
     cross_count = face_cross.shape[0]
     metric_dom = lax.all_gather(metric, "dom", axis=0, tiled=True)
-    metric_grp = lax.all_gather(metric, "grp", axis=0, tiled=True)
+    stack = jnp.stack([metric] * lax.axis_size("grp"))
+    metric_grp = jnp.concatenate(lax.all_to_all(stack, "grp", 0, 0), axis=0)
     diag_side = plain_restrictor(metric)
     diag_c = coarse_terms(diag_side, one_sided(diag_blocks, diag_side))
     diag_rows = diag_c.reshape(elem_count, square).astype(jnp.bfloat16)

time: 172 us -> 172 us (level)
  blocking collectives: 48.4 us -> 42 us
  starting transfers between devices: 0.08 us -> 6 us
  waiting for transfers between devices: 54.5 us -> 48.8 us
  other arithmetic: 14.3 us -> 17.4 us
  local copies, waits for them, and re-layouts: 15.2 us -> 17.3 us
    all_gather x1 -> x0, blocking collectives: 14.6 us -> none  [per_device(): metric_grp = lax.all_gather(metric, 'grp', axis=0, tiled=True)]
    all_to_all x0 -> x1, starting transfers between devices: none -> 5.96 us  [per_device(): metric_grp = jnp.concatenate(lax.all_to_all(stack, 'grp', 0, 0), axis=0)]
    all_gather x1, blocking collectives: 13.5 us -> 19.2 us  [per_device(): cross_got = lax.all_gather(cross_packet, 'grp', axis=0)]
    all_gather x1, waiting for transfers between devices: 54.4 us -> 48.8 us  [per_device(): face_all = lax.all_gather(face_packet, 'dom', axis=0)]
    all_gather x1, blocking collectives: 20.3 us -> 22.8 us  [per_device(): metric_dom = lax.all_gather(metric, 'dom', axis=0, tiled=True)]
    select_n x2, other arithmetic: 1.9 us -> 4.05 us  [restrictor(): shaped = jnp.where(bits % 2 == 1, jnp.flip(shaped, 3), shaped)]
  transfers between devices with their start and end apart: 2 -> 3, of which waited for: 1 -> 1; matrix products, arithmetic and copies ran while one was open for 18% -> 23% of each run, Pallas kernels for 0% -> 0%
where the time goes in v1:
time: 172 us; the launch traced here: 171 us
  waiting for transfers between devices  48.8 us (28%)
  blocking collectives  42 us (24%)
  matrix products  24.9 us (14%)
  other arithmetic  17.4 us (10%)
  local copies, waits for them, and re-layouts  17.3 us (10%)
  between operations  14.5 us (8%)
  starting transfers between devices  6 us (3%)
    all_gather x1, waiting for transfers between devices, per_device(): face_all = lax.all_gather(face_packet, 'dom', axis=0)  48.8 us
    all_gather x1, blocking collectives, per_device(): metric_dom = lax.all_gather(metric, 'dom', axis=0, tiled=True)  22.8 us
    all_gather x1, blocking collectives, per_device(): cross_got = lax.all_gather(cross_packet, 'grp', axis=0)  19.2 us
    dot_general x3, matrix products, coarse_terms(): jnp.einsum('rci,rdi->rcd', row_side, products, preferred_element_type=jnp...  17.5 us
    reshape x1, local copies, waits for them, and re-layouts, per_device(): coarse_face = face.reshape(group_width * elem_count, 3 * square)  8.64 us
    dot_general x1, matrix products, per_device(): face = jnp.dot(onehot, contrib, preferred_element_type=jnp.float32)  5.96 us
    all_to_all x1, starting transfers between devices, per_device(): metric_grp = jnp.concatenate(lax.all_to_all(stack, 'grp', 0, 0), axis=0)  5.96 us
    select_n x2, other arithmetic, restrictor(): shaped = jnp.where(bits % 2 == 1, jnp.flip(shaped, 3), shaped)  4.05 us
  transfers between devices with their start and end apart: 3, of which 1 were waited for; matrix products, arithmetic and copies ran while one was open for 23% of the time, Pallas kernels for 0%

profile of v1, /device:TPU:1, one launch (start us, length us, event | category | flops | bytes accessed | tf_op | source)
XLA Modules:
  0.0 170.9 jit_solution(14262000413329774232)
XLA Ops:
  7.2 1.4 stack.14
  8.6 6.0 %all-to-all-start = ((f32[8,16,384]{2,1,0:T(8,128)}), f32[8,16,384]{2,1,0:T(8,128)S(1)}, u32[]{:S(2)}, u32[]{:S(2)}) async-start(f32[8,16,384]{2,1,0:T(8,128)} %stack.14), calls=%async_computation | async-start | bytes 393216 | tf_op jit(solution)/shard_map/all_to_all | solution.py:81
  14.8 0.1 mul.188
  14.9 0.1 broadcast_multiply_fusion.3
  15.0 0.1 mul.191
  15.1 4.3 %fusion.26 = bf16[16,48,48]{2,1,0:T(8,128)(2,1)S(1)} fusion(bf16[16,384,384]{2,1,0:T(8,128)(2,1)} %param.12, f32[48,384]{1,0:T(8,128)S(1)} %mul.191, f32[16,384]{1,0:T(8,128)} %param.15), kind=kOutput, calls=%fused_computation.30 | convolution fusion | flops 256315392 | bytes 4890624 | tf_op jit(solution)/shard_map/rci,rdi->rcd/dot_general | solution.py:47
  19.4 0.8 convert_element_type.104
  20.4 0.1 copy.31
  20.5 22.8 %all_gather.19 = f32[256,384]{1,0:T(8,128)} all-gather(f32[16,384]{1,0:T(8,128)S(1)} %copy-done.1), channel_id=1, replica_groups=mesh['grp'=8,'dom'=16] {'dom'}, dimensions={0}, use_global_device_ids=true | all-gather | bytes 417792 | tf_op jit(solution)/shard_map/all_gather | solution.py:79
  43.3 0.1 mul.206
  43.6 0.4 fusion.43
  44.1 0.1 copy.36
  44.1 0.1 convert_element_type.118
  44.3 0.4 fusion.39
  44.7 1.9 %broadcast_multiply_fusion.1 = bf16[16,48,6,4,4,4]{1,0,5,4,3,2:T(8,128)(2,1)} fusion(f32[48,6,4,4,4]{0,4,3,2,1:T(4,128)S(1)} %broadcast_multiply_fusion.2, f32[16,6,4,4,4]{0,4,3,2,1:T(4,128)S(1)} %bitcast.43), kind=kLoop, calls=%fused_computation.17 | loop fusion | flops 589824 | bytes 688128 | tf_op jit(solution)/shard_map/mul | solution.py:19
  46.6 2.1 %broadcast_multiply_fusion = bf16[32,48,6,4,4,4]{1,0,5,4,3,2:T(8,128)(2,1)S(1)} fusion(f32[48,6,4,4,4]{0,4,3,2,1:T(4,128)S(1)} %broadcast_multiply_fusion.2, f32[32,6,4,4,4]{0,4,3,2,1:T(4,128)S(1)} %bitcast.41), kind=kLoop, calls=%fused_computation.11 | loop fusion | flops 1179648 | bytes 1302528 | tf_op jit(solution)/shard_map/mul | solution.py:19
  48.8 1.3 reverse_select_fusion.2
  50.1 1.5 reverse_select_fusion.1
  51.6 1.1 fusion
  52.7 0.3 fusion.37
  53.0 8.9 %fusion.17 = bf16[32,48,48]{2,1,0:T(8,128)(2,1)} fusion(bf16[32,384,384]{2,1,0:T(8,128)(2,1)} %param.13, bf16[32,48,384]{1,0,2:T(8,128)(2,1)S(1)} %bitcast.38, f32[48,384]{1,0:T(8,128)S(1)} %mul.191, f32[32,384]{1,0:T(8,128)S(1)} %fusion.37), kind=kOutput, calls=%fused_computation.23 | convolution fusion | flops 511451136 | bytes 10887168 | tf_op jit(solution)/shard_map/rci,rdi->rcd/dot_general | solution.py:47
  61.9 2.0 %convert_element_type.111 = bf16[32,2304]{1,0:T(8,128)(2,1)} reshape(bf16[32,48,48]{2,1,0:T(8,128)(2,1)} %fusion.17) | data formatting | bytes 294912 | tf_op jit(solution)/shard_map/convert_element_type | solution.py:126
  63.9 2.8 %reverse_select_fusion.5 = bf16[16,48,6,4,4,4]{1,0,5,4,3,2:T(8,128)(2,1)S(1)} fusion(bf16[16,48,6,4,4,4]{1,0,5,4,3,2:T(8,128)(2,1)} %broadcast_multiply_fusion.1, pred[16]{0:T(512)(128)(4,1)S(1)} %get-tuple-element.15), kind=kLoop, calls=%fused_computation.6 | loop fusion | flops 294912 | bytes 1179664 | tf_op jit(solution)/shard_map/jit(_where)/select_n | solution.py:22
  66.7 0.7 reverse_select_fusion.4
  67.4 0.6 fusion.1
  68.0 0.2 fusion.42
  68.2 4.3 %fusion.27 = bf16[16,48,48]{2,1,0:T(8,128)(2,1)S(1)} fusion(bf16[16,384,384]{2,1,0:T(8,128)(2,1)} %param.14, bf16[16,48,384]{1,0,2:T(8,128)(2,1)S(1)} %bitcast.39, f32[16,384]{1,0:T(8,128)S(1)} %fusion.42, f32[48,384]{1,0:T(8,128)S(1)} %mul.191), kind=kOutput, calls=%fused_computation.31 | convolution fusion | flops 255725568 | bytes 5480448 | tf_op jit(solution)/shard_map/rci,rdi->rcd/dot_general | solution.py:47
  72.5 0.2 convert_element_type.117
  72.8 19.2 %all-gather.2 = bf16[8,17,2304]{2,1,0:T(8,128)(2,1)S(1)} all-gather(bf16[1,17,2304]{2,1,0:T(8,128)(2,1)S(1)} %maximum_bitcast_fusion.1), channel_id=2, replica_groups=mesh['grp'=8,'dom'=16] {'grp'}, dimensions={0}, use_global_device_ids=true | all-gather | bytes 705024 | tf_op jit(solution)/shard_map/all_gather | solution.py:96
  92.1 0.1 slice.27
  92.2 0.2 reduce_window_sum.11
  92.4 0.2 fusion.60
  92.6 0.2 select_reduce_fusion
  92.9 0.1 fusion.47
  93.0 0.1 copy.37
  93.2 0.1 convert_element_type.123
  93.3 0.2 convolution_convert_fusion
  93.6 0.1 reshape.531
  93.7 0.7 maximum_bitcast_fusion
  94.5 2.8 %convert_element_type.105 = f32[256,2304]{1,0:T(8,128)} convert(bf16[256,2304]{1,0:T(8,128)(2,1)} %all-gather.7.cloned.1.call-done) | non-fusion elementwise | flops 589824 | bytes 3538944 | tf_op jit(solution)/shard_map/convert_element_type | solution.py:140
  97.3 48.8 %all-gather.9.cloned.1.call-done = bf16[16,57,2304]{2,1,0:T(8,128)(2,1)} async-done(((bf16[1,57,2304]{2,1,0:T(8,128)(2,1)}), bf16[16,57,2304]{2,1,0:T(8,128)(2,1)}) %all-gather.9.cloned.1.call-update) | async-done | bytes 4202512 | tf_op jit(solution)/shard_map/all_gather | solution.py:128
  146.1 0.8 slice_convert_fusion
  146.8 0.2 slice.29
  147.0 0.2 slice.30
  147.2 0.1 select_n.198
  147.3 2.2 %slice-done = bf16[16,56,2304]{2,1,0:T(8,128)(2,1)S(1)} async-done(((bf16[16,57,2304]{2,1,0:T(8,128)(2,1)}), bf16[16,56,2304]{2,1,0:T(8,128)(2,1)S(1)}, s32[]{:S(2)}) %slice-start) | async-done | bytes 4128792 | tf_op jit(solution)/shard_map/slice | solution.py:130
  149.5 6.0 %fusion.4 = f32[768,2304]{1,0:T(8,128)} fusion(bf16[896,2304]{1,0:T(8,128)(2,1)S(1)} %bitcast.40, s32[896]{0:T(1024)S(1)} %select_n.198), kind=kOutput, calls=%fused_computation.13 | convolution fusion | flops 3171581952 | bytes 11210240 | tf_op jit(solution)/shard_map/dot_general | solution.py:139
  155.4 8.6 %reshape.533 = f32[256,6912]{1,0:T(8,128)} reshape(f32[768,2304]{1,0:T(8,128)} %fusion.4) | data formatting | bytes 14155776 | tf_op jit(solution)/shard_map/reshape | solution.py:141
  (58 shorter events, 1.0 us)
Async XLA Ops:
  8.6 59.4 %all-to-all-start = ((f32[8,16,384]{2,1,0:T(8,128)}), f32[8,16,384]{2,1,0:T(8,128)S(1)}, u32[]{:S(2)}, u32[]{:S(2)}) async-start(f32[8,16,384]{2,1,0:T(8,128)} %stack.14), calls=%async_computation | async-start | bytes 393216 | tf_op jit(solution)/shard_map/all_to_all | solution.py:81
  14.5 5.9 %copy-start.1 = (f32[16,384]{1,0:T(8,128)S(1)}, f32[16,384]{1,0:T(8,128)}, u32[]{:S(2)}) copy-start(f32[16,384]{1,0:T(8,128)} %param.15) | copy-start | bytes 73732
  14.5 79.9 %all-gather.7.cloned.1.call-start = ((), (), s32[]{:S(2)}) async-start(), calls=%async_computation.1 | async-start | bytes 1253376 | tf_op jit(solution)/shard_map/all_gather | solution.py:85
  15.0 28.5 %copy-start.3 = (s32[16]{0:T(128)S(1)}, s32[16]{0:T(128)}, u32[]{:S(2)}) copy-start(s32[16]{0:T(128)} %param.17) | copy-start | bytes 196
  15.1 28.9 %copy-start.5 = (s32[16]{0:T(128)S(1)}, s32[16]{0:T(128)}, u32[]{:S(2)}) copy-start(s32[16]{0:T(128)} %param.19) | copy-start | bytes 196
  15.1 28.9 %copy-start.7 = (s32[16,1]{0,1:T(1,128)S(1)}, s32[16,1]{0,1:T(1,128)}, u32[]{:S(2)}) copy-start(s32[16,1]{0,1:T(1,128)} %param.21) | copy-start | bytes 196
  15.1 28.9 %copy-start.6 = (s32[16]{0:T(128)S(1)}, s32[16]{0:T(128)}, u32[]{:S(2)}) copy-start(s32[16]{0:T(128)} %param.23) | copy-start | bytes 196
  15.1 29.2 %copy-start.4 = (s32[32]{0:T(128)S(1)}, s32[32]{0:T(128)}, u32[]{:S(2)}) copy-start(s32[32]{0:T(128)} %param.16) | copy-start | bytes 388
  20.3 125.8 %all-gather.9.cloned.1.call-start = ((), (), s32[]{:S(2)}) async-start(), calls=%async_computation.2 | async-start | bytes 5013504 | tf_op jit(solution)/shard_map/all_gather | solution.py:128
  43.4 5.3 %copy-start.8 = (s32[32]{0:T(128)S(1)}, s32[32]{0:T(128)}, u32[]{:S(2)}) copy-start(s32[32]{0:T(128)} %param.18) | copy-start | bytes 388
  43.4 5.3 %copy-start.9 = (s32[32]{0:T(128)S(1)}, s32[32]{0:T(128)}, u32[]{:S(2)}) copy-start(s32[32]{0:T(128)} %param.22) | copy-start | bytes 388
  43.4 5.3 %copy-start.10 = (s32[32,1]{0,1:T(1,128)S(1)}, s32[32,1]{0,1:T(1,128)}, u32[]{:S(2)}) copy-start(s32[32,1]{0,1:T(1,128)} %param.20) | copy-start | bytes 388
  51.6 1.2 copy-start
  68.2 25.4 %copy-start.2 = (bf16[32,2304]{1,0:T(8,128)(2,1)S(1)}, bf16[32,2304]{1,0:T(8,128)(2,1)}, u32[]{:S(2)}) copy-start(bf16[32,2304]{1,0:T(8,128)(2,1)} %convert_element_type.111) | copy-start | bytes 442372
  147.3 2.2 %slice-start = ((bf16[16,57,2304]{2,1,0:T(8,128)(2,1)}), bf16[16,56,2304]{2,1,0:T(8,128)(2,1)S(1)}, s32[]{:S(2)}) async-start(bf16[16,57,2304]{2,1,0:T(8,128)(2,1)} %all-gather.9.cloned.1.call-done), calls=%async_computation.3 | async-start | bytes 8257536 | tf_op jit(solution)/shard_map/slice | solution.py:130
Sparse Core Ops, SparseCore 0:
  20.4 43.2 all-gather.6
  94.5 51.4 all-gather.8
